TPU v7x, 32 devices: a whole 2x2x4 slice. The times are simulated.
32 devices in a mesh: src: 4 (over y, core), help: 8 (over z, x).
Axes of the slice: x: 2, y: 2, z: 4, core: 2. Of those that a mesh axis runs over, the one named last changes fastest.
Arguments:
- tiles: int32 [2, 256], P(None, 'src'), may hold values from 0 to 31, as said below
- cell_slot: int32 [2, 32], replicated, may hold values from 0 to 31, as said below
- counts: int32 [32, 2], P(('src', 'help')), may hold values from 128 to 512, as said below
- src_points: bfloat16 [16384, 512], P(('src', 'help')), may hold values from -9 to 9
- tgt_points: bfloat16 [16384, 512], P(('src', 'help')), may hold values from -9 to 9
Outputs:
- source_potential: float32 [16384], P(('src', 'help'))
- target_potential: float32 [16384], P(('src', 'help'))
- transport: float32 [16384, 512], P(('src', 'help'))
Inputs may be any that keep to these rules, and one draw needn't show every extreme that they name: `tiles`: columns come in blocks of 64, block g for group g of 8 cells: a block's source cells have ids g * 8 to g * 8 + 7, its target cells lie in group g or in group g + 1 (group 4 - 1 is followed by group 0); no pair is listed twice, and every source cell and every target cell is named in some column. Each row is a permutation that keeps every cell in its group: cell c is stored at slot cell_slot[side, c], with cell_slot[side, c] // 8 equal to c // 8; slot k is rows k * 512 to k * 512 + 511 of the point arrays. `counts`: rows of a slot at and beyond its count are padding. Both ends of the range occur in each column.
All inputs are finite; a program needn't handle non-finite values.
Results may differ from a plain program's by a relative error of at most 0.004.
Values may be sent and summed in bfloat16 or wider, within the bound.
A program may use at most 192 MiB of HBM per device.

v0:
```python
import math

import jax
import jax.numpy as jnp
from jax import lax
from jax.sharding import PartitionSpec as P

ITERS = 2


EPSILON = 0.2
NEGATIVE = -1e30


def passed_along(array, axis, by):
    count = lax.axis_size(axis)
    return lax.ppermute(array, axis, [(i, (i + by) % count) for i in range(count)])


def combined_all(part, axis, combine):
    gathered = jax.tree.map(lambda a: lax.all_gather(a, axis), part)

    def take(source):
        return jax.tree.map(lambda a: lax.dynamic_index_in_dim(a, source, 0, False), gathered)

    return lax.fori_loop(
        1, lax.axis_size(axis), lambda source, state: combine(state, take(source)), take(0)
    )


def join_parts(first, second):
    highest = jnp.maximum(first[0], second[0])
    return (
        highest,
        first[1] * jnp.exp(first[0] - highest) + second[1] * jnp.exp(second[0] - highest),
    )


def lookup(cell_ids, slot_table):
    matches = cell_ids[:, None] == jnp.arange(slot_table.shape[0], dtype=jnp.int32)[None, :]
    return jnp.sum(jnp.where(matches, slot_table[None, :], 0), axis=1)


def half_norms(points, group_size, cell_rows):
    return 0.5 * jnp.sum(jnp.square(points.astype(jnp.float32)), axis=1).reshape(
        group_size, cell_rows
    )


def shards(tiles, cell_slot, counts, src_points, tgt_points):
    group_size = lax.axis_size("help")
    help_index = lax.axis_index("help")
    src_index = lax.axis_index("src")
    cell_rows = src_points.shape[0]
    width = src_points.shape[1]
    cost_scale = math.sqrt(width)
    source_all, source_counts = (src_points, counts)
    source_cells_held = 1
    own_points, own_counts = (
        lax.all_gather(tgt_points, "help", axis=0, tiled=True),
        lax.all_gather(counts, "help", axis=0, tiled=True),
    )
    next_points, next_counts = passed_along((own_points, own_counts), "src", -1)
    candidates = 2 * group_size
    positions = jnp.arange(cell_rows, dtype=jnp.int32)
    source_live = positions[None, :] < source_counts[:, 0:1]
    target_live = jnp.stack(
        [positions[None, :] < own_counts[:, 1:2], positions[None, :] < next_counts[:, 1:2]], axis=0
    )
    flat_live = target_live.reshape(candidates, cell_rows)
    source_half = half_norms(source_all, source_cells_held, cell_rows)
    target_half = jnp.stack(
        [
            half_norms(own_points, group_size, cell_rows),
            half_norms(next_points, group_size, cell_rows),
        ],
        axis=0,
    )
    flat_half = target_half.reshape(candidates, cell_rows)
    target_points = jnp.concatenate([own_points, next_points], axis=0)
    src_slot = lookup(tiles[0], cell_slot[0])
    tgt_slot = lookup(tiles[1], cell_slot[1])
    src_cells = src_slot % group_size
    tgt_cells = tgt_slot % group_size
    tgt_sides = jnp.where(tgt_slot // group_size == src_index, 0, 1)
    tgt_keys = tgt_sides * group_size + tgt_cells
    key_ids = jnp.arange(candidates, dtype=jnp.int32)
    is_mine = src_cells == help_index
    listed_keys = jnp.any(is_mine[:, None] & (tgt_keys[:, None] == key_ids[None, :]), axis=0)
    inner = lax.dot_general(
        src_points, target_points, (((1,), (1,)), ((), ())), preferred_element_type=jnp.float32
    )
    cost = (source_half[0][:, None] + flat_half.reshape(-1)[None, :] - inner) / cost_scale
    column_live = (flat_live & listed_keys[:, None]).reshape(-1)
    mask = source_live[0][:, None] & column_live[None, :]
    own_live = source_live[0]
    target_table = jnp.zeros((2, group_size, cell_rows), jnp.float32)
    source_table = jnp.zeros((source_cells_held, cell_rows), jnp.float32)
    source_own = jnp.zeros((cell_rows,), jnp.float32)
    target_own = jnp.zeros((cell_rows,), jnp.float32)
    for sweep in range(ITERS):
        row_flat_target = target_table.reshape(candidates, cell_rows)
        row_scores = jnp.where(
            mask, (row_flat_target.reshape(-1)[None, :] - cost) / EPSILON, NEGATIVE
        )
        part_max = jnp.max(row_scores, axis=1)
        part_sum = jnp.sum(jnp.exp(row_scores - part_max[:, None]), axis=1)
        row_source_own = jnp.where(own_live, -EPSILON * (part_max + jnp.log(part_sum)), 0.0)
        row_source_table = row_source_own[None, :]
        source_table = row_source_table
        source_own = row_source_own
        scores = jnp.where(mask, (source_table[0][:, None] - cost) / EPSILON, NEGATIVE)
        peaks = jnp.max(scores, axis=0)
        sums = jnp.sum(jnp.exp(scores - peaks[None, :]), axis=0)
        peaks = peaks.reshape(2, group_size, cell_rows)
        sums = sums.reshape(2, group_size, cell_rows)
        peaks, sums = combined_all((peaks, sums), "help", join_parts)
        carried_max, carried_sum = passed_along((peaks[1], sums[1]), "src", 1)
        joined = join_parts((peaks[0], sums[0]), (carried_max, carried_sum))
        target_group = jnp.where(target_live[0], -EPSILON * (joined[0] + jnp.log(joined[1])), 0.0)
        target_after = passed_along(target_group, "src", -1)
        col_target_table = jnp.stack([target_group, target_after], axis=0)
        col_target_own = target_group[help_index]
        target_table = col_target_table
        target_own = col_target_own
    flat_target = target_table.reshape(candidates, cell_rows)
    exponent = (source_table[0][:, None] + flat_target.reshape(-1)[None, :] - cost) / EPSILON
    weight = jnp.where(mask, jnp.exp(exponent), 0.0).astype(jnp.bfloat16)
    own_numerator = jnp.dot(weight, target_points, preferred_element_type=jnp.float32)
    own_denominator = jnp.sum(weight.astype(jnp.float32), axis=1)
    safe_total = jnp.where(own_live, own_denominator, 1.0)
    transport = jnp.where(own_live[:, None], own_numerator / safe_total[:, None], 0.0)
    return (source_own, target_own, transport)


def solution(mesh):
    in_specs = (
        P(None, "src"),
        P(),
        P(("src", "help"), None),
        P(("src", "help"), None),
        P(("src", "help"), None),
    )
    out_specs = (P(("src", "help")), P(("src", "help")), P(("src", "help"), None))
    return jax.shard_map(shards, mesh=mesh, in_specs=in_specs, out_specs=out_specs, check_vma=False)
```

profile of v0, /device:TPU:0, one launch (start us, length us, event | category | flops | bytes accessed | tf_op | source)
XLA Modules:
  0.0 362.0 jit_solution(11354192799630096327)
XLA Ops:
  7.2 0.0 all-gather.3.cloned.1.call-start
  7.2 0.7 all-gather.3.cloned.1.call-update
  7.9 77.7 %all-gather.3.cloned.1.call-done = bf16[4096,512]{1,0:T(8,128)(2,1)} async-done(((bf16[512,512]{1,0:T(8,128)(2,1)}), bf16[4096,512]{1,0:T(8,128)(2,1)}) %all-gather.3.cloned.1.call-update) | async-done | bytes 4194320 | tf_op jit(solution)/shard_map/all_gather | solution.py:60
  85.7 19.1 %all-gather = s32[8,1,2]{2,1,0:T(1,128)S(1)} all-gather(s32[1,1,2]{2,1,0:T(1,128)} %bitcast.156), channel_id=1, replica_groups=mesh['src'=4,'help'=8] {'help'}, dimensions={0}, use_global_device_ids=true | all-gather | bytes 72 | tf_op jit(solution)/shard_map/all_gather | solution.py:61
  104.7 0.1 copy.10
  104.8 0.7 iota_compare_fusion.6
  105.5 0.8 slice_bitcast_fusion.11
  106.2 0.8 slice_bitcast_fusion.10
  107.0 0.1 select_reduce_fusion
  107.1 0.1 fusion.30
  107.2 1.2 multiply_reduce_fusion.2
  108.5 0.1 iota_compare_fusion.4
  108.6 0.1 broadcast_bitcast_fusion
  108.7 23.3 %collective-permute-done = s32[8,2]{0,1:T(2,128)S(1)} collective-permute-done((s32[8,2]{0,1:T(2,128)S(1)}, s32[8,2]{0,1:T(2,128)S(1)}, u32[]{:S(2)}, u32[]{:S(2)}) %collective-permute-start) | collective-permute-done | bytes 96 | tf_op jit(solution)/shard_map/ppermute | solution.py:17
  132.0 0.1 iota_compare_fusion.3
  132.1 3.1 multiply_reduce_fusion.1
  135.2 4.4 %constant_dynamic-update-slice_fusion.1 = bf16[8192,512]{1,0:T(8,128)(2,1)} fusion(bf16[4096,512]{1,0:T(8,128)(2,1)} %all-gather.3.cloned.1.call-done), kind=kLoop, calls=%fused_computation.82 | loop fusion | bytes 8388608
  139.6 3.1 multiply_reduce_fusion
  142.8 4.4 %constant_dynamic-update-slice_fusion = bf16[8192,512]{1,0:T(8,128)(2,1)} fusion(bf16[8192,512]{1,0:T(8,128)(2,1)} %constant_dynamic-update-slice_fusion.1, bf16[4096,512]{1,0:T(8,128)(2,1)} %collective-permute-done.1), kind=kLoop, calls=%fused_computation.81 | loop fusion | bytes 8388608 | tf_op jit(solution)/shard_map/concatenate | solution.py:80
  147.2 10.4 %fusion.6 = (f32[512]{0:T(512)S(1)}, f32[512,8192]{0,1:T(8,128)S(1)}) fusion(pred[512]{0:T(512)(128)(4,1)S(1)} %iota_compare_fusion.6, pred[8192]{0:T(1024)(128)(4,1)S(1)} %and.81, bf16[8192,512]{1,0:T(8,128)(2,1)} %constant_dynamic-update-slice_fusion, bf16[512,512]{1,0:T(8,128)(2,1)S(1)} %copy-done.2, f32[8192]{0:T(1024)S(1)} %bitcast.153, ...), kind=kOutput, calls=%fused_computation.23 | convolution fusion | flops 4328521216 | bytes 25735680 | tf_op jit(solution)/shard_map/dot_general | solution.py:90
  157.6 7.0 %exponential_reduce_fusion.3 = f32[512]{0:T(512)S(1)} fusion(f32[512,8192]{0,1:T(8,128)S(1)} %get-tuple-element.304, f32[512]{0:T(512)S(1)} %get-tuple-element.303, pred[512]{0:T(512)(128)(4,1)S(1)} %iota_compare_fusion.6, pred[8192]{0:T(1024)(128)(4,1)S(1)} %and.81), kind=kLoop, calls=%fused_computation.22 | loop fusion | flops 25165312 | bytes 16790016 | tf_op jit(solution)/shard_map/reduce_sum | solution.py:107
  164.7 4.8 %fusion.7 = f32[8192]{0:T(1024)S(1)} fusion(f32[512,8192]{0,1:T(8,128)S(1)} %get-tuple-element.304, f32[512]{0:T(512)S(1)} %multiply_select_fusion.1, pred[512]{0:T(512)(128)(4,1)S(1)} %iota_compare_fusion.6, pred[8192]{0:T(1024)(128)(4,1)S(1)} %and.81), kind=kLoop, calls=%fused_computation.24 | loop fusion | flops 20963328 | bytes 16820736 | tf_op jit(solution)/shard_map/reduce_max | solution.py:113
  169.6 6.7 %exponential_reduce_fusion.2 = f32[8192]{0:T(1024)S(1)} fusion(f32[512,8192]{0,1:T(8,128)S(1)} %get-tuple-element.304, f32[8192]{0:T(1024)S(1)} %fusion.7, f32[512]{0:T(512)S(1)} %multiply_select_fusion.1, pred[512]{0:T(512)(128)(4,1)S(1)} %iota_compare_fusion.6, pred[8192]{0:T(1024)(128)(4,1)S(1)} %and.81), kind=kLoop, calls=%fused_computation.21 | loop fusion | flops 25157632 | bytes 16853504 | tf_op jit(solution)/shard_map/reduce_sum | solution.py:114
  176.3 30.9 %all_gather.21 = f32[8,2,8,512]{3,2,1,0:T(8,128)S(1)} all-gather(f32[1,2,8,512]{3,2,1,0:T(8,128)S(1)} %all_gather_reshape.13), channel_id=1, replica_groups=mesh['src'=4,'help'=8] {'help'}, dimensions={0}, use_global_device_ids=true | all-gather | bytes 294912 | tf_op jit(solution)/shard_map/all_gather | solution.py:21
  207.2 30.9 %all_gather.20 = f32[8,2,8,512]{3,2,1,0:T(8,128)S(1)} all-gather(f32[1,2,8,512]{3,2,1,0:T(8,128)S(1)} %all_gather_reshape.12), channel_id=1, replica_groups=mesh['src'=4,'help'=8] {'help'}, dimensions={0}, use_global_device_ids=true | all-gather | bytes 294912 | tf_op jit(solution)/shard_map/all_gather | solution.py:21
  238.1 0.4 while.34
  238.5 0.1 collective-permute-start.2
  238.5 1.4 collective-permute-start.3
  239.9 1.8 collective-permute-done.2
  241.7 0.2 collective-permute-done.3
  241.9 0.1 fusion.24
  242.0 1.4 collective-permute-done.4
  243.4 10.3 %fusion.8 = f32[512]{0:T(512)S(1)} fusion(f32[512,8192]{0,1:T(8,128)} %copy-done, f32[8192]{0:T(1024)S(1)} %bitcast.146, pred[512]{0:T(512)(128)(4,1)S(1)} %iota_compare_fusion.6, pred[8192]{0:T(1024)(128)(4,1)S(1)} %and.81), kind=kLoop, calls=%fused_computation.25 | loop fusion | flops 20971008 | bytes 16820736 | tf_op jit(solution)/shard_map/reduce_max | solution.py:106
  253.7 5.6 %exponential_reduce_fusion.1 = f32[512]{0:T(512)S(1)} fusion(f32[512,8192]{0,1:T(8,128)S(1)} %copy-done.1, f32[512]{0:T(512)S(1)} %fusion.8, f32[8192]{0:T(1024)S(1)} %bitcast.147, pred[512]{0:T(512)(128)(4,1)S(1)} %iota_compare_fusion.6, pred[8192]{0:T(1024)(128)(4,1)S(1)} %and.81), kind=kLoop, calls=%fused_computation.20 | loop fusion | flops 25165312 | bytes 16822784 | tf_op jit(solution)/shard_map/reduce_sum | solution.py:107
  259.4 4.8 %fusion.9 = f32[8192]{0:T(1024)S(1)} fusion(f32[512,8192]{0,1:T(8,128)S(1)} %copy-done.1, f32[512]{0:T(512)S(1)} %multiply_select_fusion, pred[512]{0:T(512)(128)(4,1)S(1)} %iota_compare_fusion.6, pred[8192]{0:T(1024)(128)(4,1)S(1)} %and.81), kind=kLoop, calls=%fused_computation.26 | loop fusion | flops 20963328 | bytes 16820736 | tf_op jit(solution)/shard_map/reduce_max | solution.py:113
  264.2 6.7 %exponential_reduce_fusion = f32[8192]{0:T(1024)S(1)} fusion(f32[512,8192]{0,1:T(8,128)S(1)} %copy-done.1, f32[8192]{0:T(1024)S(1)} %fusion.9, f32[512]{0:T(512)S(1)} %multiply_select_fusion, pred[512]{0:T(512)(128)(4,1)S(1)} %iota_compare_fusion.6, pred[8192]{0:T(1024)(128)(4,1)S(1)} %and.81), kind=kLoop, calls=%fused_computation.19 | loop fusion | flops 25157632 | bytes 16853504 | tf_op jit(solution)/shard_map/reduce_sum | solution.py:114
  270.9 30.9 %all_gather.23 = f32[8,2,8,512]{3,2,1,0:T(8,128)S(1)} all-gather(f32[1,2,8,512]{3,2,1,0:T(8,128)S(1)} %all_gather_reshape.15), channel_id=1, replica_groups=mesh['src'=4,'help'=8] {'help'}, dimensions={0}, use_global_device_ids=true | all-gather | bytes 294912 | tf_op jit(solution)/shard_map/all_gather | solution.py:21
  301.9 30.9 %all_gather.22 = f32[8,2,8,512]{3,2,1,0:T(8,128)S(1)} all-gather(f32[1,2,8,512]{3,2,1,0:T(8,128)S(1)} %all_gather_reshape.14), channel_id=1, replica_groups=mesh['src'=4,'help'=8] {'help'}, dimensions={0}, use_global_device_ids=true | all-gather | bytes 294912 | tf_op jit(solution)/shard_map/all_gather | solution.py:21
  332.8 0.4 while.35
  333.2 0.1 collective-permute-start.5
  333.3 1.3 collective-permute-start.6
  334.5 1.9 collective-permute-done.5
  336.4 0.2 collective-permute-done.6
  336.6 0.1 fusion.15
  336.7 0.6 constant_dynamic-slice_fusion
  337.3 0.8 collective-permute-done.7
  338.1 8.1 %convert_reduce_fusion = (f32[512]{0:T(512)S(1)}, bf16[512,8192]{0,1:T(8,128)(2,1)S(1)}) fusion(f32[512,8192]{0,1:T(8,128)} %copy-done, f32[8192]{0:T(1024)S(1)} %bitcast.148, f32[512]{0:T(512)S(1)} %multiply_select_fusion, pred[8192]{0:T(1024)(128)(4,1)S(1)} %and.81, pred[512]{0:T(512)(128)(4,1)S(1)} %iota_compare_fusion.6), kind=kLoop, calls=%fused_computation.18 | loop fusion | flops 33553920 | bytes 25211392 | tf_op jit(solution)/shard_map/reduce_sum | solution.py:130
  346.3 8.9 %fusion.10 = f32[512,512]{1,0:T(8,128)} fusion(bf16[512,8192]{0,1:T(8,128)(2,1)S(1)} %get-tuple-element.298, bf16[8192,512]{1,0:T(8,128)(2,1)} %constant_dynamic-update-slice_fusion, f32[512]{0:T(512)S(1)} %broadcast_select_fusion, pred[512]{0:T(512)(128)(4,1)S(1)} %iota_compare_fusion.6), kind=kOutput, calls=%fused_computation.30 | convolution fusion | flops 4295491584 | bytes 17828352 | tf_op jit(solution)/shard_map/dot_general | solution.py:129
  (63 shorter events, 0.8 us)
Async XLA Ops:
  7.2 140.0 %copy-start.2 = (bf16[512,512]{1,0:T(8,128)(2,1)S(1)}, bf16[512,512]{1,0:T(8,128)(2,1)}, u32[]{:S(2)}) copy-start(bf16[512,512]{1,0:T(8,128)(2,1)} %param.12) | copy-start | bytes 1572868
  7.2 78.5 %all-gather.3.cloned.1.call-start = ((), (), s32[]{:S(2)}) async-start(), calls=%async_computation | async-start | bytes 4718592 | tf_op jit(solution)/shard_map/all_gather | solution.py:60
  85.7 54.0 %collective-permute-start.1 = (bf16[4096,512]{1,0:T(8,128)(2,1)}, bf16[4096,512]{1,0:T(8,128)(2,1)}, u32[]{:S(2)}, u32[]{:S(2)}) collective-permute-start(bf16[4096,512]{1,0:T(8,128)(2,1)} %all-gather.3.cloned.1.call-done), channel_id=1, source_target_pairs={{0,24},{8,0},{16,8},{24,16},{1,25},{9,1},{17,9},{25,17},{2,26},{10... | collective-permute-start | bytes 12582920 | tf_op jit(solution)/shard_map/ppermute | solution.py:17
  104.8 27.2 %collective-permute-start = (s32[8,2]{0,1:T(2,128)S(1)}, s32[8,2]{0,1:T(2,128)S(1)}, u32[]{:S(2)}, u32[]{:S(2)}) collective-permute-start(s32[8,2]{0,1:T(2,128)S(1)} %bitcast.162), channel_id=1, source_target_pairs={{0,24},{8,0},{16,8},{24,16},{1,25},{9,1},{17,9},{25,17},{2,26},{10... | collective-permute-start | bytes 200 | tf_op jit(solution)/shard_map/ppermute | solution.py:17
  157.6 11.9 %copy-start = (f32[512,8192]{0,1:T(8,128)}, f32[512,8192]{0,1:T(8,128)S(1)}, u32[]{:S(2)}) copy-start(f32[512,8192]{0,1:T(8,128)S(1)} %get-tuple-element.304) | copy-start | bytes 50331652
  157.6 7.0 %copy-start.4 = (s32[1,2]{1,0:T(1,128)S(1)}, s32[1,2]{1,0:T(1,128)}, u32[]{:S(2)}) copy-start(s32[1,2]{1,0:T(1,128)} %param.11) | copy-start | bytes 28
  238.5 3.2 collective-permute-start.2
  238.5 3.3 collective-permute-start.3
  241.9 1.5 collective-permute-start.4
  242.0 11.7 %copy-start.1 = (f32[512,8192]{0,1:T(8,128)S(1)}, f32[512,8192]{0,1:T(8,128)}, u32[]{:S(2)}) copy-start(f32[512,8192]{0,1:T(8,128)} %copy-done) | copy-start | bytes 50331652
  259.4 78.8 %copy-start.3 = (f32[512]{0:T(512)}, f32[512]{0:T(512)S(1)}, u32[]{:S(2)}) copy-start(f32[512]{0:T(512)S(1)} %multiply_select_fusion) | copy-start | bytes 6148
  333.2 3.2 collective-permute-start.5
  333.3 3.3 collective-permute-start.6
  336.6 1.5 collective-permute-start.7
Sparse Core Ops, SparseCore 0:
  10.1 75.4 all-gather.2
where the time goes:
time: 363 us; the launch traced here: 362 us
  blocking collectives  143 us (39%)
  waiting for transfers between devices  108 us (30%)
  other arithmetic  63.1 us (17%)
  matrix products  19.3 us (5%)
  between operations  14.4 us (4%)
  local copies, waits for them, and re-layouts  11.2 us (3%)
    all_gather x4, blocking collectives, combined_all(): gathered = jax.tree.map(lambda a: lax.all_gather(a, axis), part)  124 us
    all_gather x1, waiting for transfers between devices, shards(): lax.all_gather(tgt_points, 'help', axis=0, tiled=True)  77.7 us
    ppermute x8, waiting for transfers between devices, passed_along(): lax.ppermute(array, axis, [(i, (i + by) % count) for i in range(count)])  29.6 us
    all_gather x1, blocking collectives, shards(): lax.all_gather(counts, 'help', axis=0, tiled=True)  19.1 us
    reduce_sum x2, other arithmetic, shards(): sums = jnp.sum(jnp.exp(scores - peaks[None, :]), axis=0)  13.3 us
    reduce_sum x2, other arithmetic, shards(): part_sum = jnp.sum(jnp.exp(row_scores - part_max[:, None]), axis=1)  12.6 us
    dot_general x1, matrix products, shards(): lax.dot_general(src_points, target_points, (((1,), (1,)), ((), ())), pref...  10.4 us
    reduce_max x1, other arithmetic, shards(): part_max = jnp.max(row_scores, axis=1)  10.3 us
  transfers between devices with their start and end apart: 9, of which 8 were waited for; matrix products, arithmetic and copies ran while one was open for 3% of the time, Pallas kernels for 0%

commit v1 on v0

v1 whole, which is shorter than its diff:
```python
import functools
import math

import jax
import jax.numpy as jnp
from jax import lax
from jax.experimental import pallas as pl
from jax.experimental.pallas import tpu as pltpu
from jax.sharding import PartitionSpec as P

ITERS = 2
EPSILON = 0.2
NEGATIVE = -1e30
LANES = 128
MESH = pl.DeviceIdType.MESH


def line_length(count):
    return 1 << ((count.bit_length()) // 2)


def lookup(cell_ids, slot_table):
    matches = cell_ids[:, None] == jnp.arange(slot_table.shape[0], dtype=jnp.int32)[None, :]
    return jnp.sum(jnp.where(matches, slot_table[None, :], 0), axis=1)


def kernel(
    groups, n, zs, xs, scale,
    src_ref, tgt_ref, aux_ref, tlive_ref, slive_ref, listed_ref,
    num_ref, den_ref, f_ref, g_ref,
    pts, aux, inner, peak, total, part, inbox, gbuf,
    local_sem, rp, ra, sp, sa, part_send, part_recv, g_send, g_recv,
):
    s = lax.axis_index("src")
    h = lax.axis_index("help")
    z, x = h // xs, h % xs
    nxt = (s + 1) % groups
    prv = (s + groups - 1) % groups
    rows, width = src_ref.shape
    quarters = rows // LANES

    cp = pltpu.make_async_copy(tgt_ref, pts.at[0, h], local_sem.at[0])
    ca = pltpu.make_async_copy(aux_ref, aux.at[0, h], local_sem.at[1])
    cp.start()
    ca.start()

    barrier = pltpu.get_barrier_semaphore()

    @pl.loop(0, n)
    def _(k):
        pl.semaphore_signal(barrier, inc=1, device_id={"src": nxt, "help": k}, device_id_type=MESH)
        pl.semaphore_signal(barrier, inc=1, device_id={"src": prv, "help": k}, device_id_type=MESH)

        @pl.when(k != h)
        def _():
            pl.semaphore_signal(barrier, inc=1, device_id={"src": s, "help": k}, device_id_type=MESH)

    peak[...] = jnp.full_like(peak, NEGATIVE)
    total[...] = jnp.zeros_like(total)
    den_ref[...] = jnp.zeros_like(den_ref)
    num_ref[...] = jnp.zeros_like(num_ref)

    def row_update(index, g):
        chunk = 32

        @pl.loop(0, rows // chunk, unroll=2)
        def _(r):
            at = pl.ds(pl.multiple_of(r * chunk, chunk), chunk)
            old = peak[at, :]
            vals = [
                inner[index, at, q * LANES:(q + 1) * LANES] + g[:, q * LANES:(q + 1) * LANES]
                for q in range(quarters)
            ]
            new = functools.reduce(jnp.maximum, vals, old)
            acc = total[at, :] * jnp.exp2(old - new)
            for v in vals:
                acc = acc + jnp.exp2(v - new)
            peak[at, :] = new
            total[at, :] = acc

    def row_finish():
        chunk = 64

        @pl.loop(0, rows // chunk)
        def _(r):
            at = pl.ds(pl.multiple_of(r * chunk, chunk), chunk)
            m = jnp.max(peak[at, :], axis=1, keepdims=True)
            t = jnp.sum(total[at, :] * jnp.exp2(peak[at, :] - m), axis=1, keepdims=True)
            f = -(m + jnp.log2(t))
            f_ref[at, :] = jnp.where(slive_ref[at, :] > 0, f, NEGATIVE)

    def block(side, slot):
        index = side * n + slot
        inner[index] = scale * lax.dot_general(
            src_ref[...], pts[side, slot], (((1,), (1,)), ((), ())),
            preferred_element_type=jnp.float32,
        )
        row_update(index, aux[side, slot] + listed_ref[index])

    def moves(kind, slot, side, dev):
        return (
            pltpu.make_async_remote_copy(
                src_ref=pts.at[0, slot], dst_ref=pts.at[side, slot],
                send_sem=sp.at[kind, slot], recv_sem=rp.at[side, slot],
                device_id=dev, device_id_type=MESH),
            pltpu.make_async_remote_copy(
                src_ref=aux.at[0, slot], dst_ref=aux.at[side, slot],
                send_sem=sa.at[kind, slot], recv_sem=ra.at[side, slot],
                device_id=dev, device_id_type=MESH),
        )

    def await_cell(side, slot):
        pltpu.make_async_copy(pts.at[side, slot], pts.at[side, slot], rp.at[side, slot]).wait()
        pltpu.make_async_copy(aux.at[side, slot], aux.at[side, slot], ra.at[side, slot]).wait()

    def each_move(slot, act):
        zz, xx = slot // xs, slot % xs
        mine = xx == x

        @pl.when(mine & (zz <= z) & (z + 1 < zs))
        def _():
            act(moves(0, slot, 0, {"src": s, "help": h + xs}))

        @pl.when(mine & (zz >= z) & (z >= 1))
        def _():
            act(moves(1, slot, 0, {"src": s, "help": h - xs}))

        for k in range(1, xs):
            @pl.when(mine)
            def _(k=k):
                act(moves(2 + k, slot, 0, {"src": s, "help": z * xs + (x + k) % xs}))

        act(moves(2, slot, 1, {"src": prv, "help": h}))

    def start(pair):
        for c in pair:
            c.start()

    def finish(pair):
        for c in pair:
            c.wait_send()

    cp.wait()
    ca.wait()
    pl.semaphore_wait(barrier, 3 * n - 1)

    def entry(e, dist):
        xoff = (e // 2) % xs
        low = e % 2
        far = dist - jnp.where(xoff > 0, 1, 0)
        zz = jnp.where(low == 0, z - far, z + far)
        valid = (far >= 0) & (far < zs) & (zz >= 0) & (zz < zs) & ((far > 0) | (low == 0))
        return valid, jnp.clip(zz, 0, zs - 1) * xs + (x + xoff) % xs

    @pl.loop(0, zs + 3)
    def _(d):
        @pl.loop(0, 2 * xs)
        def _(e):
            valid, slot = entry(e, d)

            @pl.when(valid)
            def _():
                @pl.when(slot != h)
                def _():
                    await_cell(0, slot)

                each_move(slot, start)

        @pl.loop(0, 4 * xs)
        def _(e):
            side = e // (2 * xs)
            valid, slot = entry(e % (2 * xs), d - 2 * side)

            @pl.when(valid)
            def _():
                @pl.when(side == 1)
                def _():
                    await_cell(1, slot)

                block(side, slot)

    def column(index):
        chunk = 64

        def step(r, state):
            m, t = state
            at = pl.ds(pl.multiple_of(r * chunk, chunk), chunk)
            f = f_ref[at, :]
            v = inner[index, at, :] + jnp.concatenate([f] * quarters, axis=1)
            v = v.reshape(chunk // 8, 8, rows)
            new = jnp.maximum(m, jnp.max(v, axis=0))
            t = t * jnp.exp2(m - new) + jnp.sum(jnp.exp2(v - new[None]), axis=0)
            return new, t

        m, t = lax.fori_loop(
            0, rows // chunk, step,
            (jnp.full((8, rows), NEGATIVE, jnp.float32), jnp.zeros((8, rows), jnp.float32)),
        )
        top = jnp.max(m, axis=0, keepdims=True)
        t = jnp.sum(t * jnp.exp2(m - top), axis=0, keepdims=True)
        return top + listed_ref[index], t

    for sweep in range(ITERS):
        row_finish()

        def part_move(side, slot):
            return pltpu.make_async_remote_copy(
                src_ref=part.at[sweep, side, slot], dst_ref=inbox.at[sweep, side, h],
                send_sem=part_send.at[sweep, side, slot], recv_sem=part_recv.at[sweep, side, h],
                device_id={"src": jnp.where(side == 0, s, nxt), "help": slot}, device_id_type=MESH)

        def g_move(side, k):
            return pltpu.make_async_remote_copy(
                src_ref=gbuf.at[sweep, 0, h], dst_ref=gbuf.at[sweep, side, h],
                send_sem=g_send.at[sweep, side, k], recv_sem=g_recv.at[sweep, side, h],
                device_id={"src": jnp.where(side == 0, s, prv), "help": k}, device_id_type=MESH)

        @pl.loop(0, 2 * n)
        def _(e):
            side = 1 - e // n
            slot = (h + 1 + e) % n
            top, t = column(side * n + slot)
            part[sweep, side, slot, 0:1, :] = top
            part[sweep, side, slot, 1:2, :] = t

            @pl.when((side == 1) | (slot != h))
            def _():
                part_move(side, slot).start()

        def join(e, state):
            m, t = state
            side, k = e // n, e % n
            m2 = inbox[sweep, side, k, 0:1, :]
            t2 = inbox[sweep, side, k, 1:2, :]
            new = jnp.maximum(m, m2)
            return new, t * jnp.exp2(m - new) + t2 * jnp.exp2(m2 - new)

        @pl.loop(0, 2 * n)
        def _(e):
            side, k = e // n, e % n

            @pl.when((side == 1) | (k != h))
            def _():
                pltpu.make_async_copy(
                    inbox.at[sweep, side, k], inbox.at[sweep, side, k],
                    part_recv.at[sweep, side, k]).wait()

        inbox[sweep, 0, h] = part[sweep, 0, h]
        m, t = lax.fori_loop(
            1, 2 * n, join, (inbox[sweep, 0, 0, 0:1, :], inbox[sweep, 0, 0, 1:2, :]), unroll=True)
        g = jnp.where(tlive_ref[...] > 0, -(m + jnp.log2(t)), NEGATIVE)
        gbuf[sweep, 0, h] = g
        g_ref[...] = g

        @pl.loop(0, 2 * n)
        def _(e):
            side, k = e // n, e % n

            @pl.when((side == 1) | (k != h))
            def _():
                g_move(side, k).start()

        if sweep + 1 < ITERS:
            peak[...] = jnp.full_like(peak, NEGATIVE)
            total[...] = jnp.zeros_like(total)

        @pl.loop(0, 2 * n)
        def _(e):
            side = e // n
            slot = (h + e) % n
            index = side * n + slot

            @pl.when((side == 1) | (slot != h))
            def _():
                pltpu.make_async_copy(
                    gbuf.at[sweep, side, slot], gbuf.at[sweep, side, slot],
                    g_recv.at[sweep, side, slot]).wait()

            g = gbuf[sweep, side, slot] + listed_ref[index]
            if sweep + 1 < ITERS:
                row_update(index, g)
            else:
                chunk = 256
                for r in range(rows // chunk):
                    at = slice(r * chunk, (r + 1) * chunk)
                    f = f_ref[at, :]
                    w = jnp.exp2(
                        (inner[index, at, :] + g) + jnp.concatenate([f] * quarters, axis=1)
                    ).astype(jnp.bfloat16)
                    num_ref[at, :] += jnp.dot(w, pts[side, slot], preferred_element_type=jnp.float32)
                    wide = w.astype(jnp.float32)
                    acc = den_ref[at, :]
                    for q in range(quarters):
                        acc = acc + wide[:, q * LANES:(q + 1) * LANES]
                    den_ref[at, :] = acc

        @pl.loop(0, 2 * n)
        def _(e):
            side, k = e // n, e % n

            @pl.when((side == 1) | (k != h))
            def _():
                part_move(side, k).wait_send()
                g_move(side, k).wait_send()

    @pl.loop(0, n)
    def _(slot):
        each_move(slot, finish)


def shards(groups, n, tiles, cell_slot, counts, src_points, tgt_points):
    help_index = lax.axis_index("help")
    src_index = lax.axis_index("src")
    rows, width = src_points.shape
    zs = line_length(n)
    xs = n // zs
    cost_scale = math.sqrt(width)
    scale = math.log2(math.e) / (EPSILON * cost_scale)
    positions = jnp.arange(rows, dtype=jnp.int32)
    source_live = positions < counts[0, 0]
    target_live = positions < counts[0, 1]
    hx = 0.5 * jnp.sum(jnp.square(src_points.astype(jnp.float32)), axis=1)
    hy = 0.5 * jnp.sum(jnp.square(tgt_points.astype(jnp.float32)), axis=1)
    aux = jnp.where(target_live, -scale * hy, NEGATIVE)[None, :]
    src_slot = lookup(tiles[0], cell_slot[0])
    tgt_slot = lookup(tiles[1], cell_slot[1])
    keys = jnp.where(tgt_slot // n == src_index, 0, n) + tgt_slot % n
    mine = src_slot % n == help_index
    listed = jnp.any(mine[:, None] & (keys[:, None] == jnp.arange(2 * n)[None, :]), axis=0)
    listed_bias = jnp.broadcast_to(jnp.where(listed, 0.0, NEGATIVE)[:, None, None], (2 * n, 1, rows))
    slive = jnp.broadcast_to(source_live.astype(jnp.float32)[:, None], (rows, LANES))
    tlive = target_live.astype(jnp.float32)[None, :]
    vmem = pl.BlockSpec(memory_space=pltpu.VMEM)
    hbm = pl.BlockSpec(memory_space=pl.ANY)
    f32 = jnp.float32
    dma = pltpu.SemaphoreType.DMA
    num, den, f, g = pl.pallas_call(
        functools.partial(kernel, groups, n, zs, xs, scale),
        out_shape=(
            jax.ShapeDtypeStruct((rows, width), f32),
            jax.ShapeDtypeStruct((rows, LANES), f32),
            jax.ShapeDtypeStruct((rows, LANES), f32),
            jax.ShapeDtypeStruct((1, rows), f32),
        ),
        in_specs=[vmem, hbm, hbm, vmem, vmem, vmem],
        out_specs=(vmem, vmem, vmem, vmem),
        scratch_shapes=[
            pltpu.VMEM((2, n, rows, width), jnp.bfloat16),
            pltpu.VMEM((2, n, 1, rows), f32),
            pltpu.VMEM((2 * n, rows, rows), f32),
            pltpu.VMEM((rows, LANES), f32),
            pltpu.VMEM((rows, LANES), f32),
            pltpu.VMEM((ITERS, 2, n, 2, rows), f32),
            pltpu.VMEM((ITERS, 2, n, 2, rows), f32),
            pltpu.VMEM((ITERS, 2, n, 1, rows), f32),
            dma((2,)),
            dma((2, n)),
            dma((2, n)),
            dma((2 + xs, n)),
            dma((2 + xs, n)),
            dma((ITERS, 2, n)),
            dma((ITERS, 2, n)),
            dma((ITERS, 2, n)),
            dma((ITERS, 2, n)),
        ],
        compiler_params=pltpu.CompilerParams(
            collective_id=0, has_side_effects=True, vmem_limit_bytes=60 * 1024 * 1024
        ),
    )(src_points, tgt_points, aux, tlive, slive, listed_bias)
    back = EPSILON * math.log(2.0)
    source_own = jnp.where(source_live, back * (f[:, 0] + scale * hx), 0.0)
    target_own = jnp.where(target_live, back * (g[0] + scale * hy), 0.0)
    safe = jnp.where(source_live, jnp.sum(den, axis=1), 1.0)
    transport = jnp.where(source_live[:, None], num / safe[:, None], 0.0)
    return (source_own, target_own, transport)


def solution(mesh):
    in_specs = (
        P(None, "src"),
        P(),
        P(("src", "help"), None),
        P(("src", "help"), None),
        P(("src", "help"), None),
    )
    out_specs = (P(("src", "help")), P(("src", "help")), P(("src", "help"), None))
    body = functools.partial(shards, mesh.shape["src"], mesh.shape["help"])
    return jax.shard_map(body, mesh=mesh, in_specs=in_specs, out_specs=out_specs, check_vma=False)
```

time: 363 us -> 123 us (0.34)
  blocking collectives: 143 us -> 0 us
  waiting for transfers between devices: 108 us -> 0 us
  Pallas kernels: 0 us -> 106 us
  other arithmetic: 63.1 us -> 9.87 us
  matrix products: 19.3 us -> 0 us
  between operations: 14.4 us -> 0.72 us
  local copies, waits for them, and re-layouts: 11.2 us -> 5.28 us
    all_gather x5 -> x0, blocking collectives: 143 us -> none  [the longest x4 124 us: combined_all(): gathered = jax.tree.map(lambda a: lax.all_gather(a, axis), part)]
    pallas_call x0 -> x1, Pallas kernels: none -> 106 us  [shards(): pl.pallas_call(functools.partial(kernel, groups, n, zs, xs, scale), out_s...]
    all_gather x1 -> x0, waiting for transfers between devices: 77.7 us -> none  [shards(): lax.all_gather(tgt_points, 'help', axis=0, tiled=True)]
    reduce_sum x8 -> x3, other arithmetic: 41.4 us -> 2.49 us  [the longest x1 1.22 us: shards(): hy = 0.5 * jnp.sum(jnp.square(tgt_points.astype(jnp.float32)), axis=1)]
    ppermute x8 -> x0, waiting for transfers between devices: 29.6 us -> none  [passed_along(): lax.ppermute(array, axis, [(i, (i + by) % count) for i in range(count)])]
    reduce_max x3 -> x0, other arithmetic: 19.9 us -> none  [the longest x1 10.3 us: shards(): part_max = jnp.max(row_scores, axis=1)]
    dot_general x2 -> x0, matrix products: 19.3 us -> none  [the longest x1 10.4 us: shards(): lax.dot_general(src_points, target_points, (((1,), (1,)), ((), ())), pref...]
    concatenate x1 -> x0, local copies, waits for them, and re-layouts: 4.43 us -> none  [shards(): target_points = jnp.concatenate([own_points, next_points], axis=0)]
  transfers between devices with their start and end apart: 9 -> 0, of which waited for: 8 -> 0; matrix products, arithmetic and copies ran while one was open for 3% -> 0% of each run, Pallas kernels for 0% -> 0%
where the time goes in v1:
time: 123 us; the launch traced here: 122 us
  Pallas kernels  106 us (86%)
  other arithmetic  9.87 us (8%)
  local copies, waits for them, and re-layouts  5.28 us (4%)
    pallas_call x1, Pallas kernels, shards(): pl.pallas_call(functools.partial(kernel, groups, n, zs, xs, scale), out_s...  106 us

profile of v1, /device:TPU:0, one launch (start us, length us, event | category | flops | bytes accessed | tf_op | source)
XLA Modules:
  0.0 122.3 jit_solution(10710763643995291856)
XLA Ops:
  0.6 1.2 multiply_reduce_fusion.1
  1.9 0.0 copy-start.3
  1.9 0.6 copy-done.3
  2.5 0.6 fusion.6
  3.1 1.1 compare_select_fusion.aux_ref
  4.2 1.1 compare_convert_fusion.tlive_ref
  5.4 0.6 fusion.5
  6.0 0.0 copy-start.4
  6.0 0.8 broadcast_in_dim.79.slive_ref
  6.8 0.0 copy-done.4
  6.8 0.0 copy-start.5
  6.9 0.7 copy-done.5
  7.5 0.1 select_reduce_fusion
  7.6 0.1 select_reduce_fusion.1
  7.7 0.1 fusion.1
  7.9 0.7 broadcast_in_dim.87.listed_ref
  8.6 0.0 copy-start
  8.6 106.4 %shard_map.76 = (f32[512,512]{1,0:T(8,128)}, f32[512,128]{1,0:T(8,128)}, f32[512,128]{1,0:T(8,128)}, f32[1,512]{1,0:T(1,128)}) custom-call(bf16[512,512]{1,0:T(8,128)(2,1)} %src_ref.1, bf16[512,512]{1,0:T(8,128)(2,1)} %tgt_ref.1, f32[1,512]{1,0:T(1,128)} %compare_select_fusion.aux_ref, f32[1,512]{1,0:T(1,128)} %compare_convert_fusion.tlive_ref, ...), custom_call_target="tpu_custom_call" | custom-call | tf_op jit(solution)/shard_map/pallas_call | solution.py:337
  115.0 0.0 copy-start.1
  115.0 1.2 slice_reduce_fusion
  116.1 0.0 copy-done
  116.2 0.2 multiply_reduce_fusion
  116.3 1.1 reduce_sum.49
  117.4 1.2 multiply_select_fusion.1
  118.7 0.0 copy-start.2
  118.7 0.7 copy-done.2
  119.3 1.1 multiply_select_fusion
  120.4 0.6 iota_compare_fusion.4
  121.1 0.0 copy-done.1
  121.1 1.2 divide_select_fusion
  (6 shorter events, 0.1 us)
Async XLA Ops:
  1.9 0.7 copy-start.3
  6.0 0.9 copy-start.4
  6.8 0.7 copy-start.5
  8.6 107.6 %copy-start = (bf16[512,512]{1,0:T(8,128)(2,1)S(1)}, bf16[512,512]{1,0:T(8,128)(2,1)}, u32[]{:S(2)}) copy-start(bf16[512,512]{1,0:T(8,128)(2,1)} %src_ref.1) | copy-start | bytes 1572868
  115.0 6.1 %copy-start.1 = (f32[512,512]{1,0:T(8,128)S(1)}, f32[512,512]{1,0:T(8,128)}, u32[]{:S(2)}) copy-start(f32[512,512]{1,0:T(8,128)} %get-tuple-element.9) | copy-start | bytes 3145732
  118.7 0.7 copy-start.2

commit v2 on v1

--- a/solution.py
+++ b/solution.py
@@ -19,16 +19,11 @@
     return 1 << ((count.bit_length()) // 2)
 
 
-def lookup(cell_ids, slot_table):
-    matches = cell_ids[:, None] == jnp.arange(slot_table.shape[0], dtype=jnp.int32)[None, :]
-    return jnp.sum(jnp.where(matches, slot_table[None, :], 0), axis=1)
-
-
 def kernel(
     groups, n, zs, xs, scale,
-    src_ref, tgt_ref, aux_ref, tlive_ref, slive_ref, listed_ref,
-    num_ref, den_ref, f_ref, g_ref,
-    pts, aux, inner, peak, total, part, inbox, gbuf,
+    tiles_ref, cell_slot_ref, counts_ref, src_ref, tgt_ref,
+    source_ref, target_ref, out_ref,
+    pts, aux, inner, peak, total, den, f_ref, hx, listed, part, inbox, gbuf,
     local_sem, rp, ra, sp, sa, part_send, part_recv, g_send, g_recv,
 ):
     s = lax.axis_index("src")
@@ -39,10 +34,8 @@
     rows, width = src_ref.shape
     quarters = rows // LANES
 
-    cp = pltpu.make_async_copy(tgt_ref, pts.at[0, h], local_sem.at[0])
-    ca = pltpu.make_async_copy(aux_ref, aux.at[0, h], local_sem.at[1])
+    cp = pltpu.make_async_copy(tgt_ref, pts.at[0, h], local_sem)
     cp.start()
-    ca.start()
 
     barrier = pltpu.get_barrier_semaphore()
 
@@ -57,8 +50,36 @@
 
     peak[...] = jnp.full_like(peak, NEGATIVE)
     total[...] = jnp.zeros_like(total)
-    den_ref[...] = jnp.zeros_like(den_ref)
-    num_ref[...] = jnp.zeros_like(num_ref)
+    den[...] = jnp.zeros_like(den)
+    out_ref[...] = jnp.zeros_like(out_ref)
+    source_count = counts_ref[0, 0]
+    target_count = counts_ref[0, 1]
+    target_live = lax.broadcasted_iota(jnp.int32, (1, rows), 1) < target_count
+
+    keys = lax.broadcasted_iota(jnp.int32, listed.shape, 0)
+
+    def mark(t, bias):
+        source_slot = cell_slot_ref[0, tiles_ref[0, t]]
+        target_slot = cell_slot_ref[1, tiles_ref[1, t]]
+        key = jnp.where(target_slot // n == s, 0, n) + target_slot % n
+        key = jnp.where(source_slot % n == h, key, 2 * n)
+        return jnp.where(keys == key, 0.0, bias)
+
+    listed[...] = lax.fori_loop(
+        0, tiles_ref.shape[1], mark, jnp.full(listed.shape, NEGATIVE, jnp.float32))
+
+    def listed_row(index):
+        row = listed[pl.ds(index, 1), :]
+        return jnp.concatenate([row] * quarters, axis=1)
+
+    def half_norms(load):
+        squares = 0.0
+        for q in range(width // LANES):
+            v = load(slice(q * LANES, (q + 1) * LANES)).astype(jnp.float32)
+            squares = squares + v * v
+        return (0.5 * scale) * jnp.sum(jnp.transpose(squares), axis=0, keepdims=True)
+
+    hx[...] = half_norms(lambda at: src_ref[:, at])
 
     def row_update(index, g):
         chunk = 32
@@ -87,7 +108,8 @@
             m = jnp.max(peak[at, :], axis=1, keepdims=True)
             t = jnp.sum(total[at, :] * jnp.exp2(peak[at, :] - m), axis=1, keepdims=True)
             f = -(m + jnp.log2(t))
-            f_ref[at, :] = jnp.where(slive_ref[at, :] > 0, f, NEGATIVE)
+            row_ids = lax.broadcasted_iota(jnp.int32, (chunk, LANES), 0) + r * chunk
+            f_ref[at, :] = jnp.where(row_ids < source_count, f, NEGATIVE)
 
     def block(side, slot):
         index = side * n + slot
@@ -95,7 +117,7 @@
             src_ref[...], pts[side, slot], (((1,), (1,)), ((), ())),
             preferred_element_type=jnp.float32,
         )
-        row_update(index, aux[side, slot] + listed_ref[index])
+        row_update(index, aux[side, slot] + listed_row(index))
 
     def moves(kind, slot, side, dev):
         return (
@@ -141,7 +163,7 @@
             c.wait_send()
 
     cp.wait()
-    ca.wait()
+    aux[0, h] = jnp.where(target_live, -half_norms(lambda at: pts[0, h, :, at]), NEGATIVE)
     pl.semaphore_wait(barrier, 3 * n - 1)
 
     def entry(e, dist):
@@ -198,7 +220,7 @@
         )
         top = jnp.max(m, axis=0, keepdims=True)
         t = jnp.sum(t * jnp.exp2(m - top), axis=0, keepdims=True)
-        return top + listed_ref[index], t
+        return top + listed_row(index), t
 
     for sweep in range(ITERS):
         row_finish()
@@ -248,9 +270,8 @@
         inbox[sweep, 0, h] = part[sweep, 0, h]
         m, t = lax.fori_loop(
             1, 2 * n, join, (inbox[sweep, 0, 0, 0:1, :], inbox[sweep, 0, 0, 1:2, :]), unroll=True)
-        g = jnp.where(tlive_ref[...] > 0, -(m + jnp.log2(t)), NEGATIVE)
+        g = jnp.where(target_live, -(m + jnp.log2(t)), NEGATIVE)
         gbuf[sweep, 0, h] = g
-        g_ref[...] = g
 
         @pl.loop(0, 2 * n)
         def _(e):
@@ -276,7 +297,7 @@
                     gbuf.at[sweep, side, slot], gbuf.at[sweep, side, slot],
                     g_recv.at[sweep, side, slot]).wait()
 
-            g = gbuf[sweep, side, slot] + listed_ref[index]
+            g = gbuf[sweep, side, slot] + listed_row(index)
             if sweep + 1 < ITERS:
                 row_update(index, g)
             else:
@@ -287,12 +308,12 @@
                     w = jnp.exp2(
                         (inner[index, at, :] + g) + jnp.concatenate([f] * quarters, axis=1)
                     ).astype(jnp.bfloat16)
-                    num_ref[at, :] += jnp.dot(w, pts[side, slot], preferred_element_type=jnp.float32)
+                    out_ref[at, :] += jnp.dot(w, pts[side, slot], preferred_element_type=jnp.float32)
                     wide = w.astype(jnp.float32)
-                    acc = den_ref[at, :]
+                    acc = den[at, :]
                     for q in range(quarters):
                         acc = acc + wide[:, q * LANES:(q + 1) * LANES]
-                    den_ref[at, :] = acc
+                    den[at, :] = acc
 
         @pl.loop(0, 2 * n)
         def _(e):
@@ -307,53 +328,53 @@
     def _(slot):
         each_move(slot, finish)
 
+    back = EPSILON * math.log(2.0)
+    source_live = lax.broadcasted_iota(jnp.int32, (1, rows), 1) < source_count
+    f_row = jnp.transpose(f_ref[...])[0:1, :]
+    source_ref[...] = jnp.where(source_live, back * (f_row + hx[...]), 0.0)
+    target_ref[...] = jnp.where(target_live, back * (gbuf[ITERS - 1, 0, h] - aux[0, h]), 0.0)
+
+    @pl.loop(0, rows // 64)
+    def _(r):
+        at = pl.ds(pl.multiple_of(r * 64, 64), 64)
+        live = lax.broadcasted_iota(jnp.int32, (64, 1), 0) + r * 64 < source_count
+        safe = jnp.where(live, jnp.sum(den[at, :], axis=1, keepdims=True), 1.0)
+        out_ref[at, :] = jnp.where(live, out_ref[at, :] / safe, 0.0)
+
 
 def shards(groups, n, tiles, cell_slot, counts, src_points, tgt_points):
-    help_index = lax.axis_index("help")
-    src_index = lax.axis_index("src")
     rows, width = src_points.shape
     zs = line_length(n)
     xs = n // zs
-    cost_scale = math.sqrt(width)
-    scale = math.log2(math.e) / (EPSILON * cost_scale)
-    positions = jnp.arange(rows, dtype=jnp.int32)
-    source_live = positions < counts[0, 0]
-    target_live = positions < counts[0, 1]
-    hx = 0.5 * jnp.sum(jnp.square(src_points.astype(jnp.float32)), axis=1)
-    hy = 0.5 * jnp.sum(jnp.square(tgt_points.astype(jnp.float32)), axis=1)
-    aux = jnp.where(target_live, -scale * hy, NEGATIVE)[None, :]
-    src_slot = lookup(tiles[0], cell_slot[0])
-    tgt_slot = lookup(tiles[1], cell_slot[1])
-    keys = jnp.where(tgt_slot // n == src_index, 0, n) + tgt_slot % n
-    mine = src_slot % n == help_index
-    listed = jnp.any(mine[:, None] & (keys[:, None] == jnp.arange(2 * n)[None, :]), axis=0)
-    listed_bias = jnp.broadcast_to(jnp.where(listed, 0.0, NEGATIVE)[:, None, None], (2 * n, 1, rows))
-    slive = jnp.broadcast_to(source_live.astype(jnp.float32)[:, None], (rows, LANES))
-    tlive = target_live.astype(jnp.float32)[None, :]
+    scale = math.log2(math.e) / (EPSILON * math.sqrt(width))
     vmem = pl.BlockSpec(memory_space=pltpu.VMEM)
+    smem = pl.BlockSpec(memory_space=pltpu.SMEM)
     hbm = pl.BlockSpec(memory_space=pl.ANY)
     f32 = jnp.float32
     dma = pltpu.SemaphoreType.DMA
-    num, den, f, g = pl.pallas_call(
+    source_own, target_own, transport = pl.pallas_call(
         functools.partial(kernel, groups, n, zs, xs, scale),
         out_shape=(
+            jax.ShapeDtypeStruct((1, rows), f32),
+            jax.ShapeDtypeStruct((1, rows), f32),
             jax.ShapeDtypeStruct((rows, width), f32),
-            jax.ShapeDtypeStruct((rows, LANES), f32),
-            jax.ShapeDtypeStruct((rows, LANES), f32),
-            jax.ShapeDtypeStruct((1, rows), f32),
         ),
-        in_specs=[vmem, hbm, hbm, vmem, vmem, vmem],
-        out_specs=(vmem, vmem, vmem, vmem),
+        in_specs=[smem, smem, smem, vmem, hbm],
+        out_specs=(vmem, vmem, vmem),
         scratch_shapes=[
             pltpu.VMEM((2, n, rows, width), jnp.bfloat16),
             pltpu.VMEM((2, n, 1, rows), f32),
             pltpu.VMEM((2 * n, rows, rows), f32),
             pltpu.VMEM((rows, LANES), f32),
             pltpu.VMEM((rows, LANES), f32),
+            pltpu.VMEM((rows, LANES), f32),
+            pltpu.VMEM((rows, LANES), f32),
+            pltpu.VMEM((1, rows), f32),
+            pltpu.VMEM((2 * n, LANES), f32),
             pltpu.VMEM((ITERS, 2, n, 2, rows), f32),
             pltpu.VMEM((ITERS, 2, n, 2, rows), f32),
             pltpu.VMEM((ITERS, 2, n, 1, rows), f32),
-            dma((2,)),
+            dma,
             dma((2, n)),
             dma((2, n)),
             dma((2 + xs, n)),
@@ -366,13 +387,8 @@
         compiler_params=pltpu.CompilerParams(
             collective_id=0, has_side_effects=True, vmem_limit_bytes=60 * 1024 * 1024
         ),
-    )(src_points, tgt_points, aux, tlive, slive, listed_bias)
-    back = EPSILON * math.log(2.0)
-    source_own = jnp.where(source_live, back * (f[:, 0] + scale * hx), 0.0)
-    target_own = jnp.where(target_live, back * (g[0] + scale * hy), 0.0)
-    safe = jnp.where(source_live, jnp.sum(den, axis=1), 1.0)
-    transport = jnp.where(source_live[:, None], num / safe[:, None], 0.0)
-    return (source_own, target_own, transport)
+    )(tiles, cell_slot, counts, src_points, tgt_points)
+    return (source_own.reshape(rows), target_own.reshape(rows), transport)
 
 
 def solution(mesh):

time: 123 us -> 112 us (0.911)
  other arithmetic: 9.87 us -> 0 us
    select_n x5 -> x0, other arithmetic: 4.65 us -> none  [the longest x1 1.21 us: shards(): source_own = jnp.where(source_live, back * (f[:, 0] + scale * hx), 0.0)]
    reduce_sum x5 -> x0, other arithmetic: 2.67 us -> none  [the longest x1 1.22 us: shards(): hy = 0.5 * jnp.sum(jnp.square(tgt_points.astype(jnp.float32)), axis=1)]
    unnamed x12 -> x7, local copies, waits for them, and re-layouts: 1.99 us -> 4.17 us
    convert_element_type x2 -> x0, other arithmetic: 1.76 us -> none  [the longest x1 1.13 us: shards(): tlive = target_live.astype(jnp.float32)[None, :]]
    slice x2 -> x0, local copies, waits for them, and re-layouts: 1.75 us -> none  [the longest x1 1.18 us: shards(): source_own = jnp.where(source_live, back * (f[:, 0] + scale * hx), 0.0)]
    broadcast_in_dim x3 -> x0, local copies, waits for them, and re-layouts: 1.53 us -> none  [the longest x1 0.84 us: shards(): jnp.broadcast_to(source_live.astype(jnp.float32)[:, None], (rows, LANES))]
where the time goes in v2:
time: 112 us
  Pallas kernels  107 us (96%)
  local copies, waits for them, and re-layouts  4.17 us (4%)
    pallas_call x1, Pallas kernels, shards(): pl.pallas_call(functools.partial(kernel, groups, n, zs, xs, scale), out_s...  107 us
    unnamed x7, local copies, waits for them, and re-layouts  4.17 us

profile of v2, /device:TPU:0, one launch (start us, length us, event | category | flops | bytes accessed | tf_op | source)
XLA Modules:
  0.0 111.9 jit_solution(16347632340001248924)
XLA Ops:
  0.6 107.1 %shard_map.76 = (f32[1,512]{1,0:T(1,128)}, f32[1,512]{1,0:T(1,128)}, f32[512,512]{1,0:T(8,128)}) custom-call(s32[2,64]{1,0:T(2,128)} %tiles_ref.1, s32[2,32]{1,0:T(2,128)} %cell_slot_ref.1, s32[1,2]{1,0:T(1,128)} %counts_ref.1, bf16[512,512]{1,0:T(8,128)(2,1)} %src_ref.1, bf16[512,512]{1,0:T(8,128)(2,1)} %tgt_ref.1), custom_call_target="tpu_custom_call" | custom-call | tf_op jit(solution)/shard_map/pallas_call | solution.py:355
  107.7 0.0 copy-start.1
  107.7 0.7 copy-done.1
  108.4 0.0 copy-start
  108.4 0.6 copy.11
  109.0 0.1 copy-done
  109.1 0.6 copy.12
  109.6 2.3 %copy.13 = f32[512,512]{1,0:T(8,128)} copy(f32[512,512]{1,0:T(8,128)} %get-tuple-element.14) | data formatting | bytes 2097152
Async XLA Ops:
  107.7 0.7 copy-start.1
  108.4 0.7 copy-start

commit v3 on v2

--- a/solution.py
+++ b/solution.py
@@ -12,6 +12,7 @@
 EPSILON = 0.2
 NEGATIVE = -1e30
 LANES = 128
+PIECES = 2
 MESH = pl.DeviceIdType.MESH
 
 
@@ -34,19 +35,88 @@
     rows, width = src_ref.shape
     quarters = rows // LANES
 
-    cp = pltpu.make_async_copy(tgt_ref, pts.at[0, h], local_sem)
-    cp.start()
+    piece_rows = rows // PIECES
+
+    def local(p):
+        return pltpu.make_async_copy(
+            tgt_ref.at[pl.ds(p * piece_rows, piece_rows), :], pts.at[0, h, p], local_sem.at[p])
+
+    for p in range(PIECES):
+        local(p).start()
 
     barrier = pltpu.get_barrier_semaphore()
 
-    @pl.loop(0, n)
-    def _(k):
-        pl.semaphore_signal(barrier, inc=1, device_id={"src": nxt, "help": k}, device_id_type=MESH)
-        pl.semaphore_signal(barrier, inc=1, device_id={"src": prv, "help": k}, device_id_type=MESH)
-
-        @pl.when(k != h)
+    def greet(**dev):
+        pl.semaphore_signal(barrier, inc=1, device_id=dev, device_id_type=MESH)
+
+    greet(src=nxt, help=h)
+    greet(src=prv, help=h)
+    for k in range(1, xs):
+        greet(src=s, help=z * xs + (x + k) % xs)
+
+    @pl.when(z + 1 < zs)
+    def _():
+        greet(src=s, help=h + xs)
+
+    @pl.when(z >= 1)
+    def _():
+        greet(src=s, help=h - xs)
+
+    @pl.when((z >= 1) & (z + 1 < zs))
+    def _():
+        pl.semaphore_wait(barrier, 3 + xs)
+
+    @pl.when((z < 1) | (z + 1 >= zs))
+    def _():
+        pl.semaphore_wait(barrier, 2 + xs)
+
+    def move(kind, slot, what, side, dev):
+        if what is None:
+            return pltpu.make_async_remote_copy(
+                src_ref=aux.at[0, slot], dst_ref=aux.at[side, slot],
+                send_sem=sa.at[kind, slot], recv_sem=ra.at[side, slot],
+                device_id=dev, device_id_type=MESH)
+        return pltpu.make_async_remote_copy(
+            src_ref=pts.at[0, slot, what], dst_ref=pts.at[side, slot, what],
+            send_sem=sp.at[kind, slot, what], recv_sem=rp.at[side, slot, what],
+            device_id=dev, device_id_type=MESH)
+
+    def await_piece(side, slot, p):
+        ref = pts.at[side, slot, p]
+        pltpu.make_async_copy(ref, ref, rp.at[side, slot, p]).wait()
+
+    def await_aux(side, slot):
+        ref = aux.at[side, slot]
+        pltpu.make_async_copy(ref, ref, ra.at[side, slot]).wait()
+
+    def each_move(slot, what, act):
+        zz, xx = slot // xs, slot % xs
+        mine = xx == x
+
+        @pl.when(mine & (zz <= z) & (z + 1 < zs))
         def _():
-            pl.semaphore_signal(barrier, inc=1, device_id={"src": s, "help": k}, device_id_type=MESH)
+            act(move(0, slot, what, 0, {"src": s, "help": h + xs}))
+
+        @pl.when(mine & (zz >= z) & (z >= 1))
+        def _():
+            act(move(1, slot, what, 0, {"src": s, "help": h - xs}))
+
+        for k in range(1, xs):
+            @pl.when(mine)
+            def _(k=k):
+                act(move(2 + k, slot, what, 0, {"src": s, "help": z * xs + (x + k) % xs}))
+
+        act(move(2, slot, what, 1, {"src": prv, "help": h}))
+
+    def start(copy):
+        copy.start()
+
+    def finish(copy):
+        copy.wait_send()
+
+    for p in range(PIECES):
+        local(p).wait()
+        each_move(h, p, start)
 
     peak[...] = jnp.full_like(peak, NEGATIVE)
     total[...] = jnp.zeros_like(total)
@@ -84,9 +154,8 @@
     def row_update(index, g):
         chunk = 32
 
-        @pl.loop(0, rows // chunk, unroll=2)
-        def _(r):
-            at = pl.ds(pl.multiple_of(r * chunk, chunk), chunk)
+        for r in range(rows // chunk):
+            at = slice(r * chunk, (r + 1) * chunk)
             old = peak[at, :]
             vals = [
                 inner[index, at, q * LANES:(q + 1) * LANES] + g[:, q * LANES:(q + 1) * LANES]
@@ -114,57 +183,14 @@
     def block(side, slot):
         index = side * n + slot
         inner[index] = scale * lax.dot_general(
-            src_ref[...], pts[side, slot], (((1,), (1,)), ((), ())),
+            src_ref[...], pts[side, slot].reshape(rows, width), (((1,), (1,)), ((), ())),
             preferred_element_type=jnp.float32,
         )
         row_update(index, aux[side, slot] + listed_row(index))
 
-    def moves(kind, slot, side, dev):
-        return (
-            pltpu.make_async_remote_copy(
-                src_ref=pts.at[0, slot], dst_ref=pts.at[side, slot],
-                send_sem=sp.at[kind, slot], recv_sem=rp.at[side, slot],
-                device_id=dev, device_id_type=MESH),
-            pltpu.make_async_remote_copy(
-                src_ref=aux.at[0, slot], dst_ref=aux.at[side, slot],
-                send_sem=sa.at[kind, slot], recv_sem=ra.at[side, slot],
-                device_id=dev, device_id_type=MESH),
-        )
-
-    def await_cell(side, slot):
-        pltpu.make_async_copy(pts.at[side, slot], pts.at[side, slot], rp.at[side, slot]).wait()
-        pltpu.make_async_copy(aux.at[side, slot], aux.at[side, slot], ra.at[side, slot]).wait()
-
-    def each_move(slot, act):
-        zz, xx = slot // xs, slot % xs
-        mine = xx == x
-
-        @pl.when(mine & (zz <= z) & (z + 1 < zs))
-        def _():
-            act(moves(0, slot, 0, {"src": s, "help": h + xs}))
-
-        @pl.when(mine & (zz >= z) & (z >= 1))
-        def _():
-            act(moves(1, slot, 0, {"src": s, "help": h - xs}))
-
-        for k in range(1, xs):
-            @pl.when(mine)
-            def _(k=k):
-                act(moves(2 + k, slot, 0, {"src": s, "help": z * xs + (x + k) % xs}))
-
-        act(moves(2, slot, 1, {"src": prv, "help": h}))
-
-    def start(pair):
-        for c in pair:
-            c.start()
-
-    def finish(pair):
-        for c in pair:
-            c.wait_send()
-
-    cp.wait()
-    aux[0, h] = jnp.where(target_live, -half_norms(lambda at: pts[0, h, :, at]), NEGATIVE)
-    pl.semaphore_wait(barrier, 3 * n - 1)
+    aux[0, h] = jnp.where(
+        target_live, -half_norms(lambda at: pts[0, h, :, :, at].reshape(rows, LANES)), NEGATIVE)
+    each_move(h, None, start)
 
     def entry(e, dist):
         xoff = (e // 2) % xs
@@ -176,17 +202,20 @@
 
     @pl.loop(0, zs + 3)
     def _(d):
-        @pl.loop(0, 2 * xs)
-        def _(e):
-            valid, slot = entry(e, d)
-
-            @pl.when(valid)
-            def _():
-                @pl.when(slot != h)
+        @pl.loop(0, PIECES * 2 * xs)
+        def _(e):
+            p = e // (2 * xs)
+            valid, slot = entry(e % (2 * xs), d)
+
+            @pl.when(valid & (slot != h))
+            def _():
+                await_piece(0, slot, p)
+                each_move(slot, p, start)
+
+                @pl.when(p == PIECES - 1)
                 def _():
-                    await_cell(0, slot)
-
-                each_move(slot, start)
+                    await_aux(0, slot)
+                    each_move(slot, None, start)
 
         @pl.loop(0, 4 * xs)
         def _(e):
@@ -197,27 +226,27 @@
             def _():
                 @pl.when(side == 1)
                 def _():
-                    await_cell(1, slot)
+                    for p in range(PIECES):
+                        await_piece(1, slot, p)
+                    await_aux(1, slot)
 
                 block(side, slot)
 
     def column(index):
         chunk = 64
 
-        def step(r, state):
-            m, t = state
-            at = pl.ds(pl.multiple_of(r * chunk, chunk), chunk)
+        def scores(r):
+            at = slice(r * chunk, (r + 1) * chunk)
             f = f_ref[at, :]
             v = inner[index, at, :] + jnp.concatenate([f] * quarters, axis=1)
-            v = v.reshape(chunk // 8, 8, rows)
-            new = jnp.maximum(m, jnp.max(v, axis=0))
-            t = t * jnp.exp2(m - new) + jnp.sum(jnp.exp2(v - new[None]), axis=0)
-            return new, t
-
-        m, t = lax.fori_loop(
-            0, rows // chunk, step,
-            (jnp.full((8, rows), NEGATIVE, jnp.float32), jnp.zeros((8, rows), jnp.float32)),
-        )
+            return v.reshape(chunk // 8, 8, rows)
+
+        m = jnp.max(scores(0), axis=0)
+        for r in range(1, rows // chunk):
+            m = jnp.maximum(m, jnp.max(scores(r), axis=0))
+        t = jnp.sum(jnp.exp2(scores(0) - m[None]), axis=0)
+        for r in range(1, rows // chunk):
+            t = t + jnp.sum(jnp.exp2(scores(r) - m[None]), axis=0)
         top = jnp.max(m, axis=0, keepdims=True)
         t = jnp.sum(t * jnp.exp2(m - top), axis=0, keepdims=True)
         return top + listed_row(index), t
@@ -308,7 +337,7 @@
                     w = jnp.exp2(
                         (inner[index, at, :] + g) + jnp.concatenate([f] * quarters, axis=1)
                     ).astype(jnp.bfloat16)
-                    out_ref[at, :] += jnp.dot(w, pts[side, slot], preferred_element_type=jnp.float32)
+                    out_ref[at, :] += jnp.dot(w, pts[side, slot].reshape(rows, width), preferred_element_type=jnp.float32)
                     wide = w.astype(jnp.float32)
                     acc = den[at, :]
                     for q in range(quarters):
@@ -326,7 +355,9 @@
 
     @pl.loop(0, n)
     def _(slot):
-        each_move(slot, finish)
+        for p in range(PIECES):
+            each_move(slot, p, finish)
+        each_move(slot, None, finish)
 
     back = EPSILON * math.log(2.0)
     source_live = lax.broadcasted_iota(jnp.int32, (1, rows), 1) < source_count
@@ -362,7 +393,7 @@
         in_specs=[smem, smem, smem, vmem, hbm],
         out_specs=(vmem, vmem, vmem),
         scratch_shapes=[
-            pltpu.VMEM((2, n, rows, width), jnp.bfloat16),
+            pltpu.VMEM((2, n, PIECES, rows // PIECES, width), jnp.bfloat16),
             pltpu.VMEM((2, n, 1, rows), f32),
             pltpu.VMEM((2 * n, rows, rows), f32),
             pltpu.VMEM((rows, LANES), f32),
@@ -374,10 +405,10 @@
             pltpu.VMEM((ITERS, 2, n, 2, rows), f32),
             pltpu.VMEM((ITERS, 2, n, 2, rows), f32),
             pltpu.VMEM((ITERS, 2, n, 1, rows), f32),
-            dma,
+            dma((PIECES,)),
+            dma((2, n, PIECES)),
             dma((2, n)),
-            dma((2, n)),
-            dma((2 + xs, n)),
+            dma((2 + xs, n, PIECES)),
             dma((2 + xs, n)),
             dma((ITERS, 2, n)),
             dma((ITERS, 2, n)),

time: 112 us -> 103 us (0.920)
  Pallas kernels: 107 us -> 97.7 us
    pallas_call x1, Pallas kernels: 107 us -> 97.7 us  [shards(): pl.pallas_call(functools.partial(kernel, groups, n, zs, xs, scale), out_s...]
where the time goes in v3:
time: 103 us; the launch traced here: 102 us
  Pallas kernels  97.7 us (95%)
  local copies, waits for them, and re-layouts  4.17 us (4%)
    pallas_call x1, Pallas kernels, shards(): pl.pallas_call(functools.partial(kernel, groups, n, zs, xs, scale), out_s...  97.7 us
    unnamed x7, local copies, waits for them, and re-layouts  4.17 us

profile of v3, /device:TPU:0, one launch (start us, length us, event | category | flops | bytes accessed | tf_op | source)
XLA Modules:
  0.0 102.5 jit_solution(6598211767422990432)
XLA Ops:
  0.6 97.7 %shard_map.76 = (f32[1,512]{1,0:T(1,128)}, f32[1,512]{1,0:T(1,128)}, f32[512,512]{1,0:T(8,128)}) custom-call(s32[2,64]{1,0:T(2,128)} %tiles_ref.1, s32[2,32]{1,0:T(2,128)} %cell_slot_ref.1, s32[1,2]{1,0:T(1,128)} %counts_ref.1, bf16[512,512]{1,0:T(8,128)(2,1)} %src_ref.1, bf16[512,512]{1,0:T(8,128)(2,1)} %tgt_ref.1), custom_call_target="tpu_custom_call" | custom-call | tf_op jit(solution)/shard_map/pallas_call | solution.py:386
  98.3 0.0 copy-start.1
  98.3 0.7 copy-done.1
  99.0 0.0 copy-start
  99.0 0.6 copy.11
  99.6 0.1 copy-done
  99.7 0.6 copy.12
  100.2 2.3 %copy.13 = f32[512,512]{1,0:T(8,128)} copy(f32[512,512]{1,0:T(8,128)} %get-tuple-element.14) | data formatting | bytes 2097152
Async XLA Ops:
  98.3 0.7 copy-start.1
  99.0 0.7 copy-start

commit v4 on v3

--- a/solution.py
+++ b/solution.py
@@ -200,7 +200,7 @@
         valid = (far >= 0) & (far < zs) & (zz >= 0) & (zz < zs) & ((far > 0) | (low == 0))
         return valid, jnp.clip(zz, 0, zs - 1) * xs + (x + xoff) % xs
 
-    @pl.loop(0, zs + 3)
+    @pl.loop(0, zs + 2)
     def _(d):
         @pl.loop(0, PIECES * 2 * xs)
         def _(e):
@@ -220,7 +220,7 @@
         @pl.loop(0, 4 * xs)
         def _(e):
             side = e // (2 * xs)
-            valid, slot = entry(e % (2 * xs), d - 2 * side)
+            valid, slot = entry(e % (2 * xs), d - side)
 
             @pl.when(valid)
             def _():

time: 103 us -> 100 us (0.971)
  Pallas kernels: 97.7 us -> 95.3 us
    pallas_call x1, Pallas kernels: 97.7 us -> 95.3 us  [shards(): pl.pallas_call(functools.partial(kernel, groups, n, zs, xs, scale), out_s...]
where the time goes in v4:
time: 100 us
  Pallas kernels  95.3 us (95%)
  local copies, waits for them, and re-layouts  4.17 us (4%)
    pallas_call x1, Pallas kernels, shards(): pl.pallas_call(functools.partial(kernel, groups, n, zs, xs, scale), out_s...  95.3 us
    unnamed x7, local copies, waits for them, and re-layouts  4.17 us

profile of v4, /device:TPU:0, one launch (start us, length us, event | category | flops | bytes accessed | tf_op | source)
XLA Modules:
  0.0 100.2 jit_solution(3742518204313746507)
XLA Ops:
  0.6 95.3 %shard_map.76 = (f32[1,512]{1,0:T(1,128)}, f32[1,512]{1,0:T(1,128)}, f32[512,512]{1,0:T(8,128)}) custom-call(s32[2,64]{1,0:T(2,128)} %tiles_ref.1, s32[2,32]{1,0:T(2,128)} %cell_slot_ref.1, s32[1,2]{1,0:T(1,128)} %counts_ref.1, bf16[512,512]{1,0:T(8,128)(2,1)} %src_ref.1, bf16[512,512]{1,0:T(8,128)(2,1)} %tgt_ref.1), custom_call_target="tpu_custom_call" | custom-call | tf_op jit(solution)/shard_map/pallas_call | solution.py:386
  96.0 0.0 copy-start.1
  96.0 0.7 copy-done.1
  96.7 0.0 copy-start
  96.7 0.6 copy.11
  97.2 0.1 copy-done
  97.3 0.6 copy.12
  97.9 2.3 %copy.13 = f32[512,512]{1,0:T(8,128)} copy(f32[512,512]{1,0:T(8,128)} %get-tuple-element.14) | data formatting | bytes 2097152
Async XLA Ops:
  96.0 0.7 copy-start.1
  96.7 0.7 copy-start
